TPU v7x, 128 devices: a whole 4x4x4 slice. The times are simulated.
128 devices in a mesh: dp: 16 (over y_hi, x, core), tensor: 8 (over z, y_lo).
Axes of the slice: x: 4, y: 4 (y_hi: 2, y_lo: 2; y = y_hi * 2 + y_lo), z: 4, core: 2. Of those that a mesh axis runs over, the one named last changes fastest.
Arguments:
- inputs: bfloat16 [2048, 8192], P('dp', 'tensor'), may hold values from -6 to 6
- out_grad: bfloat16 [2048, 8192], P('dp', 'tensor'), may hold values from -6 to 6
- weights: bfloat16 [3, 768, 128, 128], P(None, 'tensor'), may hold values from -0.1875 to 0.1875
- block_index: int32 [3, 768, 2], P(None, 'tensor'), may hold values from 0 to 63, as said below
- block_counts: int32 [8, 3], P('tensor'), may hold values from 38 to 96, as said below
- first_moment: float32 [3, 768, 128, 128], P(None, ('tensor', 'dp')), may hold values from -120 to 120
- second_moment: float32 [3, 768, 128, 128], P(None, ('tensor', 'dp')), may hold values from 100 to 10000
Outputs:
- outputs: bfloat16 [2048, 8192], P('dp', 'tensor')
- input_grad: bfloat16 [2048, 8192], P('dp', 'tensor')
- update: float32 [3, 768, 128, 128], P(None, ('tensor', 'dp'))
Inputs may be any that keep to these rules, and one draw needn't show every extreme that they name: block_index[k, t * 96 + j, 0] is a feature block (below 64) and block_index[k, t * 96 + j, 1] a hidden block of tensor index t (below 14); the 96 slots of one matrix on one tensor index name distinct blocks. block_counts[t, k] live slots of matrix k on tensor index t; for each matrix some tensor index has exactly 96.
All inputs are finite; a program needn't handle non-finite values.
Results may differ from a plain program's by a relative error of at most 0.013.
Values may be sent and summed in bfloat16 or wider, within the bound.
A program may use at most 128 MiB of HBM per device.

v0:
```python
import functools

import jax
import jax.numpy as jnp
from jax import lax
from jax.experimental import pallas as pl
from jax.experimental.pallas import tpu as pltpu
from jax.sharding import PartitionSpec as P

MESH = pl.DeviceIdType.MESH
EPSILON = 1e-08
HB = 14
CAP = 96
DB = 64
B = 128
ZERO = 192

L_X, L_OG, L_W, L_M, L_OUT = 0, 8, 16, 19, 21
N_LOCAL = 24
R_X, R_OG, R_O, R_I, R_G, R_CORE = 0, 8, 16, 23, 30, 51
N_REMOTE = 63


def slot_lists(block_index, counts):
    feature, hid = block_index[:, :, 0], block_index[:, :, 1]
    slot = jnp.arange(CAP, dtype=jnp.int32)
    live = slot[None, :] < counts[0][:, None]

    def padded(target, source, weight, alive):
        pad = 2 * CAP - target.shape[0]
        packed = weight | (source << 9) | (jnp.where(alive, target, DB) << 16)
        return jnp.pad(packed, (0, pad), constant_values=DB << 16)

    both = lambda a, b: jnp.concatenate([a, b])
    packed = jnp.stack(
        [
            padded(hid[0], feature[0], slot, live[0]),
            padded(hid[1], feature[1], slot + CAP, live[1]),
            padded(hid[2], feature[2], slot + 2 * CAP, live[2]),
            padded(feature[2], hid[2], slot + 2 * CAP, live[2]),
            padded(
                both(feature[0], feature[1]),
                both(hid[0], hid[1] + HB),
                both(slot, slot + CAP),
                both(live[0], live[1]),
            ),
        ]
    )
    place = jnp.arange(2 * CAP, dtype=jnp.int32)
    key = (packed >> 16) * 256 + place[None, :]
    rank = jnp.sum((key[:, None, :] < key[:, :, None]).astype(jnp.int32), axis=2)
    ordered = jnp.sum(
        jnp.where(rank[:, None, :] == place[None, :, None], packed[:, None, :], 0), axis=2
    )
    target = ordered >> 16
    same = jnp.pad((target[:, 1:] == target[:, :-1]).astype(jnp.int32), ((0, 0), (1, 0)))
    lists = (ordered & 0xFFFF) | (same << 16)
    group = jnp.arange(DB, dtype=jnp.int32)
    upto = jnp.sum((key[:, None, :] < (group[None, :, None] + 1) * 256).astype(jnp.int32), axis=2)
    before = jnp.sum((key[:, None, :] < group[None, :, None] * 256).astype(jnp.int32), axis=2)
    base = jnp.array([0, CAP, CAP, 0, 0], jnp.int32)
    lasts = jnp.where(upto > before, upto - 1 + base[:, None], ZERO)
    pairs = feature | (hid << 8)
    return lists, lasts, pairs


def kernel(
    inputs, out_grad, weights, lists, lasts, pairs, counts, first, second,
    out_o, out_i, out_u,
    xb, gb, wb, sums, gate, up, hidden, rows, ob, ib, grads, core_in,
    ra_o, rb_o, rm_o, ra_g, rb_g, rm_g, mom,
    lsem, ssem, rsem,
):
    d, t = lax.axis_index("dp"), lax.axis_index("tensor")
    core, px, yh = d % 2, (d // 2) % 4, d // 8
    z, yl = t // 2, t % 2
    dev_core = (d + 1 - 2 * core, t)
    dev_xp = (yh * 8 + ((px + 1) % 4) * 2 + core, t)
    dev_xm = (yh * 8 + ((px + 3) % 4) * 2 + core, t)
    dev_yh = ((1 - yh) * 8 + px * 2 + core, t)
    dev_zp = (d, ((z + 1) % 4) * 2 + yl)
    dev_zm = (d, ((z + 3) % 4) * 2 + yl)
    dev_yl = (d, t + 1 - 2 * yl)

    def local(src, dst, sem):
        return pltpu.make_async_copy(src, dst, lsem.at[sem])

    def remote(src, dst, sem, dev):
        return pltpu.make_async_remote_copy(
            src_ref=src, dst_ref=dst, send_sem=ssem.at[sem], recv_sem=rsem.at[sem],
            device_id=dev, device_id_type=MESH,
        )

    sent = []

    def send(copy):
        copy.start()
        sent.append(copy)

    for i in range(8):
        local(inputs.at[:, pl.ds(i * B, B)], xb.at[t * 8 + i], L_X + i).start()
    for i in range(8):
        local(out_grad.at[:, pl.ds(i * B, B)], gb.at[t * 8 + i], L_OG + i).start()
    barrier = pltpu.get_barrier_semaphore()
    for dev in (dev_core, dev_xp, dev_xm, dev_yh, dev_zp, dev_zm, dev_yl):
        pl.semaphore_signal(barrier, inc=1, device_id=dev, device_id_type=MESH)
    for k in range(3):
        local(weights.at[k], wb.at[pl.ds(k * CAP, CAP)], L_W + k).start()
    local(first, mom.at[0], L_M).start()
    local(second, mom.at[1], L_M + 1).start()
    sums[ZERO] = jnp.zeros((B, B), jnp.float32)
    pl.semaphore_wait(barrier, 7)

    class Gather:
        def __init__(self, buf, base):
            chunk = lambda zz, yy, lo=0, n=8: buf.at[pl.ds((((zz + 4) % 4) * 2 + yy) * 8 + lo, n)]
            mk = lambda ref, sem, dev: remote(ref, ref, base + sem, dev)
            other = 1 - yl
            self.a = mk(chunk(z, yl), 0, dev_yl)
            self.bp = mk(chunk(z, yl), 1, dev_zp)
            self.bm = mk(chunk(z, yl), 2, dev_zm)
            self.cp = mk(chunk(z, other), 3, dev_zp)
            self.cm = mk(chunk(z, other), 4, dev_zm)
            self.dp = mk(chunk(z - 1, yl, 0, 4), 5, dev_zp)
            self.dm = mk(chunk(z + 1, yl, 4, 4), 6, dev_zm)
            self.e = mk(chunk(z + 2, yl), 7, dev_yl)

    class Reduce:
        def __init__(self, part, pos, pair, dev_p, dev_m, dev_pair, ra, rb, rm, base):
            nxt, opp, prv = (pos + 1) % 4, (pos + 2) % 4, (pos + 3) % 4
            self.part, self.pos, self.pair = part, pos, pair
            self.nxt, self.prv = nxt, prv
            self.ra, self.rb, self.rm = ra, rb, rm
            self.ap = remote(part(0, opp), ra.at[0], base, dev_p)
            self.am = remote(part(1, opp), ra.at[1], base + 1, dev_m)
            self.bp0 = remote(part(0, nxt), rb.at[0, 0], base + 2, dev_p)
            self.bp1 = remote(part(1, nxt), rb.at[0, 1], base + 3, dev_p)
            self.bm0 = remote(part(0, prv), rb.at[1, 0], base + 4, dev_m)
            self.bm1 = remote(part(1, prv), rb.at[1, 1], base + 5, dev_m)
            self.m = remote(part(1 - pair, pos), rm, base + 6, dev_pair)
            self.n = rm.shape[0]

        def start(self):
            send(self.ap)
            send(self.am)
            send(self.bp1)
            send(self.bm0)

        def relay(self):
            self.ap.wait_recv()
            add_into(self.part(0, self.nxt), self.ra.at[0], self.n)
            send(self.bp0)
            self.am.wait_recv()
            add_into(self.part(1, self.prv), self.ra.at[1], self.n)
            send(self.bm1)

        def cross(self):
            for b in (self.bp0, self.bp1, self.bm0, self.bm1):
                b.wait_recv()
            far = 1 - self.pair
            mine = self.part(far, self.pos)

            def body(i, carry):
                v = mine[i].astype(jnp.float32) + self.rb[0, far, i].astype(jnp.float32)
                mine[i] = (v + self.rb[1, far, i].astype(jnp.float32)).astype(jnp.bfloat16)
                return carry

            lax.fori_loop(0, self.n, body, 0)
            send(self.m)

        def total(self, i):
            mine = self.part(self.pair, self.pos)
            v = mine[i].astype(jnp.float32) + self.rb[0, self.pair, i].astype(jnp.float32)
            v = v + self.rb[1, self.pair, i].astype(jnp.float32)
            return v + self.rm[i].astype(jnp.float32)

    def add_into(dst, src, n):
        def body(i, carry):
            dst[i] = (dst[i].astype(jnp.float32) + src[i].astype(jnp.float32)).astype(jnp.bfloat16)
            return carry

        lax.fori_loop(0, n, body, 0)

    def products(which, lo, hi, left, base, back):
        dims = (((1,), (1,)), ((), ())) if back else (((1,), (0,)), ((), ()))
        unroll = 8

        def body(i, acc):
            for u in range(unroll):
                j = lo + i * unroll + u
                v = lists[which, j]
                prod = lax.dot_general(
                    left[(v >> 9) & 127], wb[v & 511], dims, preferred_element_type=jnp.float32
                )
                acc = acc * (v >> 16).astype(jnp.float32) + prod
                sums[base + j] = acc
            return acc

        return lambda acc: lax.fori_loop(0, (hi - lo) // unroll, body, acc)

    zero = jnp.zeros((B, B), jnp.float32)

    def gather_blocks(which, dst):
        def body(i, carry):
            dst[i] = sums[lasts[which, i]].astype(jnp.bfloat16)
            return carry

        lax.fori_loop(0, DB, body, 0, unroll=4)

    def slot_grads(k, parity, left, right, left_hidden, row_base):
        def body(b, carry):
            s0 = ((b % 2) * 8 + (b // 2) * 2 + parity) * 6
            for u in range(6):
                v = pairs[k, s0 + u]
                f, h = v & 255, v >> 8
                i, j = (h, f) if left_hidden else (f, h + row_base)
                g = lax.dot_general(
                    left[i], right[j], (((0,), (0,)), ((), ())), preferred_element_type=jnp.float32
                )
                grads[parity, k * 48 + b * 6 + u] = g.astype(jnp.bfloat16)
            return carry

        lax.fori_loop(0, 8, body, 0)

    def core_piece(k, n):
        x = (px + (2, 1, 3, 0)[n]) % 4
        at = pl.ds(k * 48 + x * 12, 12)
        return remote(grads.at[1 - core, at], core_in.at[at], R_CORE + k * 4 + n, dev_core), at

    def core_send(k):
        for n in range(4):
            send(core_piece(k, n)[0])

    def core_add(k, n):
        copy, at = core_piece(k, n)
        copy.wait_recv()
        add_into(grads.at[core, at], core_in.at[at], 12)

    def reduce_grads(k):
        part = lambda j, r: grads.at[core, pl.ds(k * 48 + r * 12 + j * 6, 6)]
        return Reduce(
            part, px, yh, dev_xp, dev_xm, dev_yh, ra_g.at[k], rb_g.at[k], rm_g.at[k], R_G + 7 * k
        )

    def reduce_rows(buf, which, base):
        part = lambda j, r: buf.at[pl.ds((r * 2 + j) * 8, 8)]
        return Reduce(
            part, z, yl, dev_zp, dev_zm, dev_yl, ra_o.at[which], rb_o.at[which], rm_o.at[which], base
        )

    gx, gg = Gather(xb, R_X), Gather(gb, R_OG)
    for i in range(8):
        local(inputs.at[:, pl.ds(i * B, B)], xb.at[t * 8 + i], L_X + i).wait()
    send(gx.a)
    send(gx.bp)
    send(gx.bm)
    for i in range(8):
        local(out_grad.at[:, pl.ds(i * B, B)], gb.at[t * 8 + i], L_OG + i).wait()
    send(gg.a)
    gx.a.wait_recv()
    send(gx.cp)
    send(gx.cm)
    gx.bp.wait_recv()
    send(gx.dp)
    gx.bm.wait_recv()
    send(gx.dm)
    send(gg.bp)
    send(gg.bm)
    gx.dp.wait_recv()
    gx.dm.wait_recv()
    send(gx.e)
    gg.a.wait_recv()
    send(gg.cp)
    send(gg.cm)
    for k in range(3):
        local(weights.at[k], wb.at[pl.ds(k * CAP, CAP)], L_W + k).wait()
    gx.cp.wait_recv()
    gx.cm.wait_recv()
    gx.e.wait_recv()

    products(0, 0, CAP, xb, 0, False)(zero)
    gg.bp.wait_recv()
    send(gg.dp)
    gg.bm.wait_recv()
    send(gg.dm)
    products(1, 0, CAP, xb, CAP, False)(zero)

    def forward(h, carry):
        g, u = sums[lasts[0, h]], sums[lasts[1, h]]
        gate[h], up[h] = g, u
        hidden[h] = (g * jax.nn.sigmoid(g) * u).astype(jnp.bfloat16)
        return carry

    lax.fori_loop(0, HB, forward, 0)
    gg.dp.wait_recv()
    gg.dm.wait_recv()
    send(gg.e)

    products(3, 0, CAP, hidden, 0, False)(zero)
    gather_blocks(3, ob)
    red_o = reduce_rows(ob, 0, R_O)
    red_o.start()
    gg.cp.wait_recv()
    gg.cm.wait_recv()
    gg.e.wait_recv()

    slot_grads(2, 1 - core, hidden, gb, True, 0)
    core_send(2)
    slot_grads(2, core, hidden, gb, True, 0)
    red_g = [reduce_grads(k) for k in range(3)]
    for n in range(3):
        core_add(2, n)
    red_g[2].start()
    core_add(2, 3)
    products(2, 0, CAP, gb, CAP, True)(zero)

    def backward(h, carry):
        g, u, hg = gate[h], up[h], sums[lasts[2, h]]
        sig = jax.nn.sigmoid(g)
        rows[h] = (hg * u * sig * (1.0 + g * (1.0 - sig))).astype(jnp.bfloat16)
        rows[h + HB] = (hg * (g * sig)).astype(jnp.bfloat16)
        return carry

    lax.fori_loop(0, HB, backward, 0)
    red_o.relay()
    slot_grads(0, 1 - core, xb, rows, False, 0)
    core_send(0)
    red_g[2].relay()
    slot_grads(0, core, xb, rows, False, 0)
    for n in range(3):
        core_add(0, n)
    red_g[0].start()
    core_add(0, 3)
    slot_grads(1, 1 - core, xb, rows, False, HB)
    core_send(1)
    slot_grads(1, core, xb, rows, False, HB)
    red_o.cross()
    red_g[0].relay()
    for n in range(3):
        core_add(1, n)
    red_g[1].start()
    core_add(1, 3)
    red_g[2].cross()
    products(4, 0, 2 * CAP, rows, 0, True)(zero)
    gather_blocks(4, ib)
    red_i = reduce_rows(ib, 1, R_I)
    red_i.start()
    red_g[1].relay()
    red_o.m.wait_recv()

    def finish_rows(red, out):
        for i in range(8):
            out[:, i * B : (i + 1) * B] = red.total(i).astype(jnp.bfloat16)

    finish_rows(red_o, out_o)

    def finish_grads(k):
        red = red_g[k]
        red.m.wait_recv()
        count = counts[0, k]

        def body(i, carry):
            g = red.total(i)
            alive = (d * 6 + i < count).astype(jnp.float32)
            m = 0.9 * mom[0, k, i] + 0.1 * g
            v = 0.95 * mom[1, k, i] + 0.05 * g * g
            out_u[k, i] = alive * m / (jnp.sqrt(v) + EPSILON)
            return carry

        lax.fori_loop(0, 6, body, 0)

    local(first, mom.at[0], L_M).wait()
    local(second, mom.at[1], L_M + 1).wait()
    finish_grads(2)
    red_i.relay()
    red_g[0].cross()
    red_i.cross()
    finish_grads(0)
    red_i.m.wait_recv()
    finish_rows(red_i, out_i)
    red_g[1].cross()
    finish_grads(1)
    for copy in sent:
        copy.wait_send()


def local_step(inputs, out_grad, weights, block_index, block_counts, first_moment, second_moment):
    lists, lasts, pairs = slot_lists(block_index, block_counts)
    any_, smem, vmem = (
        pl.BlockSpec(memory_space=s) for s in (pl.ANY, pltpu.SMEM, pltpu.VMEM)
    )
    f32, bf16 = jnp.float32, jnp.bfloat16
    blocks = lambda *n, dtype=bf16: pltpu.VMEM((*n, B, B), dtype)
    dma = pltpu.SemaphoreType.DMA
    return pl.pallas_call(
        kernel,
        out_shape=(
            jax.ShapeDtypeStruct(inputs.shape, bf16),
            jax.ShapeDtypeStruct(inputs.shape, bf16),
            jax.ShapeDtypeStruct(first_moment.shape, f32),
        ),
        in_specs=[any_, any_, any_, smem, smem, smem, smem, any_, any_],
        out_specs=[vmem, vmem, vmem],
        scratch_shapes=[
            blocks(DB),
            blocks(DB),
            blocks(3 * CAP),
            blocks(ZERO + 1, dtype=f32),
            blocks(HB, dtype=f32),
            blocks(HB, dtype=f32),
            blocks(HB),
            blocks(2 * HB),
            blocks(DB),
            blocks(DB),
            blocks(2, 3 * 48),
            blocks(3 * 48),
            blocks(2, 2, 8),
            blocks(2, 2, 2, 8),
            blocks(2, 8),
            blocks(3, 2, 6),
            blocks(3, 2, 2, 6),
            blocks(3, 6),
            blocks(2, 3, 6, dtype=f32),
            dma((N_LOCAL,)),
            dma((N_REMOTE,)),
            dma((N_REMOTE,)),
        ],
        compiler_params=pltpu.CompilerParams(
            collective_id=0, has_side_effects=True, vmem_limit_bytes=63_000_000
        ),
    )(inputs, out_grad, weights, lists, lasts, pairs, block_counts, first_moment, second_moment)


def solution(mesh):
    in_specs = (
        P("dp", "tensor"),
        P("dp", "tensor"),
        P(None, "tensor", None, None),
        P(None, "tensor", None),
        P("tensor", None),
        P(None, ("tensor", "dp"), None, None),
        P(None, ("tensor", "dp"), None, None),
    )
    out_specs = (P("dp", "tensor"), P("dp", "tensor"), P(None, ("tensor", "dp"), None, None))
    return jax.shard_map(local_step, mesh=mesh, in_specs=in_specs, out_specs=out_specs, check_vma=False)
```

profile of v0, /device:TPU:0, one launch (start us, length us, event | category | flops | bytes accessed | tf_op | source)
XLA Modules:
  0.0 126.1 jit_solution(10717172626155779464)
XLA Ops:
  0.6 0.7 iota_compare_fusion.1
  1.4 0.8 slice_bitcast_fusion.2
  2.1 0.8 fusion.10
  2.9 0.1 fusion.2
  3.1 0.8 fusion.15
  3.8 0.6 fusion.1.pairs
  4.4 0.3 convert_reduce_fusion.1
  4.7 0.4 convert_reduce_fusion
  5.2 0.3 select_reduce_fusion
  5.4 1.3 %add_select_fusion.lasts = s32[5,64]{1,0:T(8,128)} fusion(s32[5,64]{1,0:T(8,128)S(1)} %get-tuple-element.4, s32[5,64]{1,0:T(8,128)S(1)} %get-tuple-element.3, s32[5]{0:T(128)} %constant.13.clone), kind=kLoop, calls=%fused_computation.8 | loop fusion | flops 1280 | bytes 3860 | tf_op jit(solution)/shard_map/jit(_where)/select_n | solution.py:62
  6.8 0.1 slice_compare_fusion
  6.8 0.7 shift-left_or_fusion.lists
  7.5 112.8 %shard_map.103 = (bf16[128,1024]{1,0:T(8,128)(2,1)}, bf16[128,1024]{1,0:T(8,128)(2,1)}, f32[3,6,128,128]{3,2,1,0:T(8,128)}) custom-call(bf16[128,1024]{1,0:T(8,128)(2,1)} %inputs.1, bf16[128,1024]{1,0:T(8,128)(2,1)} %out_grad.1, bf16[3,96,128,128]{3,2,1,0:T(8,128)(2,1)} %weights.1, s32[5,192]{1,0:T(8,128)} %shift-left_or_fusion.lists, ...), custom_call_target="tpu_custom_call" | custom-call | tf_op jit(solution)/shard_map/pallas_call | solution.py:395
  120.4 1.7 %copy.26 = bf16[128,1024]{1,0:T(8,128)(2,1)} copy(bf16[128,1024]{1,0:T(8,128)(2,1)} %get-tuple-element.22) | data formatting | bytes 524288
  122.0 1.7 %copy.27 = bf16[128,1024]{1,0:T(8,128)(2,1)} copy(bf16[128,1024]{1,0:T(8,128)(2,1)} %get-tuple-element.23) | data formatting | bytes 524288
  123.7 2.4 %copy.28 = f32[3,6,128,128]{3,2,1,0:T(8,128)} copy(f32[3,6,128,128]{3,2,1,0:T(8,128)} %get-tuple-element.24) | data formatting | bytes 2359296
  (11 shorter events, 0.1 us)
where the time goes:
time: 126 us
  Pallas kernels  113 us (90%)
  local copies, waits for them, and re-layouts  7.3 us (6%)
  other arithmetic  5.25 us (4%)
    pallas_call x1, Pallas kernels, local_step(): pl.pallas_call(kernel, out_shape=(jax.ShapeDtypeStruct(inputs.shape, bf16...  113 us
    unnamed x3, local copies, waits for them, and re-layouts  5.72 us

commit v1 on v0

v1 whole, which is shorter than its diff:
```python
import functools

import jax
import jax.numpy as jnp
from jax import lax
from jax.experimental import pallas as pl
from jax.experimental.pallas import tpu as pltpu
from jax.sharding import PartitionSpec as P

MESH = pl.DeviceIdType.MESH
EPSILON = 1e-08
HB = 14
CAP = 96
DB = 64
B = 128
PAIRS = (56, 56, 56, 80, 128)
BASE = (0, 64, 64, 0, 0)
ZERO = 128
NO_SLOT = 3 * CAP

L_X, L_OG, L_W, L_M, L_IDX, L_LIST = 0, 8, 16, 19, 21, 23
N_LOCAL = 25
R_X, R_OG, R_O, R_I, R_GA, R_GB, R_CORE = 0, 8, 16, 23, 30, 51, 66
N_REMOTE = 84


def kernel(
    inputs, out_grad, weights, index, counts, first, second,
    out_o, out_i, out_u,
    xb, gb, wb, sums, gate, up, hidden, rows, ob, ib, grads, core_in,
    ra_o, rb_o, rm_o, ra_g, rb_g, rm_g, ya_g, yr_g, yb_g, mom,
    index_v, pairs, lists_v, lists,
    lsem, ssem, rsem,
):
    d, t = lax.axis_index("dp"), lax.axis_index("tensor")
    core, px, yh = d % 2, (d // 2) % 4, d // 8
    z, yl = t // 2, t % 2
    dev_core = (d + 1 - 2 * core, t)
    dev_xp = (yh * 8 + ((px + 1) % 4) * 2 + core, t)
    dev_xm = (yh * 8 + ((px + 3) % 4) * 2 + core, t)
    dev_yh = ((1 - yh) * 8 + px * 2 + core, t)
    dev_zp = (d, ((z + 1) % 4) * 2 + yl)
    dev_zm = (d, ((z + 3) % 4) * 2 + yl)
    dev_yl = (d, t + 1 - 2 * yl)

    def local(src, dst, sem):
        return pltpu.make_async_copy(src, dst, lsem.at[sem])

    def remote(src, dst, sem, dev):
        return pltpu.make_async_remote_copy(
            src_ref=src, dst_ref=dst, send_sem=ssem.at[sem], recv_sem=rsem.at[sem],
            device_id=dev, device_id_type=MESH,
        )

    sent = []

    def send(copy):
        copy.start()
        sent.append(copy)

    for i in range(8):
        local(inputs.at[:, pl.ds(i * B, B)], xb.at[t * 8 + i], L_X + i).start()
    for i in range(8):
        local(out_grad.at[:, pl.ds(i * B, B)], gb.at[t * 8 + i], L_OG + i).start()
    barrier = pltpu.get_barrier_semaphore()
    for dev in (dev_core, dev_xp, dev_xm, dev_yh, dev_zp, dev_zm, dev_yl):
        pl.semaphore_signal(barrier, inc=1, device_id=dev, device_id_type=MESH)
    for k in range(3):
        local(weights.at[k], wb.at[pl.ds(k * CAP, CAP)], L_W + k).start()
    local(first, mom.at[0], L_M).start()
    local(second, mom.at[1], L_M + 1).start()
    local(index, index_v, L_IDX).start()
    local(index, pairs, L_IDX + 1).start()
    wb[NO_SLOT] = jnp.zeros((B, B), jnp.bfloat16)
    sums[ZERO] = jnp.zeros((B, B), jnp.float32)
    pl.semaphore_wait(barrier, 7)

    class Gather:
        def __init__(self, buf, base):
            chunk = lambda zz, yy, lo=0, n=8: buf.at[pl.ds((((zz + 4) % 4) * 2 + yy) * 8 + lo, n)]
            mk = lambda ref, sem, dev: remote(ref, ref, base + sem, dev)
            other = 1 - yl
            self.a = mk(chunk(z, yl), 0, dev_yl)
            self.bp = mk(chunk(z, yl), 1, dev_zp)
            self.bm = mk(chunk(z, yl), 2, dev_zm)
            self.cp = mk(chunk(z, other), 3, dev_zp)
            self.cm = mk(chunk(z, other), 4, dev_zm)
            self.dp = mk(chunk(z - 1, yl, 0, 4), 5, dev_zp)
            self.dm = mk(chunk(z + 1, yl, 4, 4), 6, dev_zm)
            self.e = mk(chunk(z + 2, yl), 7, dev_yl)

    class Reduce:
        def __init__(self, part, pos, pair, dev_p, dev_m, dev_pair, ra, rb, rm, base):
            nxt, opp, prv = (pos + 1) % 4, (pos + 2) % 4, (pos + 3) % 4
            self.part, self.pos, self.pair = part, pos, pair
            self.nxt, self.prv = nxt, prv
            self.ra, self.rb, self.rm = ra, rb, rm
            self.ap = remote(part(0, opp), ra.at[0], base, dev_p)
            self.am = remote(part(1, opp), ra.at[1], base + 1, dev_m)
            self.bp0 = remote(part(0, nxt), rb.at[0, 0], base + 2, dev_p)
            self.bp1 = remote(part(1, nxt), rb.at[0, 1], base + 3, dev_p)
            self.bm0 = remote(part(0, prv), rb.at[1, 0], base + 4, dev_m)
            self.bm1 = remote(part(1, prv), rb.at[1, 1], base + 5, dev_m)
            self.m = remote(part(1 - pair, pos), rm, base + 6, dev_pair)
            self.n = rm.shape[0]

        def start(self):
            send(self.ap)
            send(self.am)

        def more(self):
            send(self.bp1)
            send(self.bm0)

        def relay(self):
            self.ap.wait_recv()
            add_into(self.part(0, self.nxt), self.ra.at[0], self.n)
            send(self.bp0)
            self.am.wait_recv()
            add_into(self.part(1, self.prv), self.ra.at[1], self.n)
            send(self.bm1)

        def cross(self):
            for b in (self.bp0, self.bp1, self.bm0, self.bm1):
                b.wait_recv()
            far = 1 - self.pair
            mine = self.part(far, self.pos)

            def body(i, carry):
                v = mine[i].astype(jnp.float32) + self.rb[0, far, i].astype(jnp.float32)
                mine[i] = (v + self.rb[1, far, i].astype(jnp.float32)).astype(jnp.bfloat16)
                return carry

            lax.fori_loop(0, self.n, body, 0)
            send(self.m)

        def total(self, i):
            mine = self.part(self.pair, self.pos)
            v = mine[i].astype(jnp.float32) + self.rb[0, self.pair, i].astype(jnp.float32)
            v = v + self.rb[1, self.pair, i].astype(jnp.float32)
            return v + self.rm[i].astype(jnp.float32)

    def add_into(dst, src, n):
        def body(i, carry):
            dst[i] = (dst[i].astype(jnp.float32) + src[i].astype(jnp.float32)).astype(jnp.bfloat16)
            return carry

        lax.fori_loop(0, n, body, 0)

    def products(which, lo, hi, left, back):
        dims = (((1,), (1,)), ((), ())) if back else (((1,), (0,)), ((), ()))
        unroll, base = 8, BASE[which]

        def body(i, acc):
            for u in range(unroll):
                j = lo + i * unroll + u
                v, w = lists[which, 2 * j], lists[which, 2 * j + 1]
                prod = lax.dot_general(
                    jnp.concatenate([left[(v >> 9) & 127], left[(w >> 9) & 127]], axis=1),
                    jnp.concatenate([wb[v & 511], wb[w & 511]], axis=1 if back else 0),
                    dims,
                    preferred_element_type=jnp.float32,
                )
                acc = acc * (v >> 16).astype(jnp.float32) + prod
                sums[base + j] = acc
            return acc

        return lambda acc: lax.fori_loop(0, (hi - lo) // unroll, body, acc)

    zero = jnp.zeros((B, B), jnp.float32)

    def gather_blocks(which, dst):
        def body(i, carry):
            dst[i] = sums[lists[5 + which, i]].astype(jnp.bfloat16)
            return carry

        lax.fori_loop(0, DB, body, 0, unroll=4)

    def slot_grads(k, parity, left, right, left_hidden, row_base):
        def body(b, carry):
            x, y = b // 2, b % 2
            s0 = (y * 8 + x * 2 + parity) * 6
            for u in range(6):
                f, h = pairs[k, 0, s0 + u], pairs[k, 1, s0 + u]
                i, j = (h, f) if left_hidden else (f, h + row_base)
                g = lax.dot_general(
                    left[i], right[j], (((0,), (0,)), ((), ())), preferred_element_type=jnp.float32
                )
                at = b * 4 + u if u < 4 else 28 + (y * 4 + x) * 2 + u
                grads[parity, k * 48 + at] = g.astype(jnp.bfloat16)
            return carry

        lax.fori_loop(0, 8, body, 0)

    def core_piece(k, n):
        nxt, opp, prv = (px + 1) % 4, (px + 2) % 4, (px + 3) % 4
        first_block = (opp * 8, 32 + (1 - yh) * 8, nxt * 8, prv * 8, 32 + yh * 8, px * 8)[n]
        at = pl.ds(k * 48 + first_block, 8)
        return remote(grads.at[1 - core, at], core_in.at[at], R_CORE + k * 6 + n, dev_core), at

    def core_send(k):
        for n in range(6):
            send(core_piece(k, n)[0])

    def core_add(k, n):
        copy, at = core_piece(k, n)
        copy.wait_recv()
        add_into(grads.at[core, at], core_in.at[at], 8)

    def reduce_grads(k):
        part = lambda j, r: grads.at[core, pl.ds(k * 48 + (r * 2 + j) * 4, 4)]
        return Reduce(
            part, px, yh, dev_xp, dev_xm, dev_yh, ra_g.at[k], rb_g.at[k], rm_g.at[k], R_GA + 7 * k
        )

    class PairFirst:
        def __init__(self, k):
            nxt, opp, prv = (px + 1) % 4, (px + 2) % 4, (px + 3) % 4
            at = lambda y, x, j, n: grads.at[core, pl.ds(k * 48 + 32 + (y * 4 + x) * 2 + j, n)]
            base = R_GB + 5 * k
            self.mine, self.got = at(yh, 0, 0, 8), ya_g.at[k]
            self.y = remote(at(1 - yh, 0, 0, 8), ya_g.at[k], base, dev_yh)
            self.ap = remote(at(yh, opp, 0, 1), yr_g.at[k, 0], base + 1, dev_xp)
            self.am = remote(at(yh, opp, 1, 1), yr_g.at[k, 1], base + 2, dev_xm)
            self.bp = remote(at(yh, nxt, 0, 2), yb_g.at[k, 0], base + 3, dev_xp)
            self.bm = remote(at(yh, prv, 0, 2), yb_g.at[k, 1], base + 4, dev_xm)
            self.for_p, self.for_m, self.last = at(yh, nxt, 0, 1), at(yh, prv, 1, 1), at(yh, px, 0, 2)
            self.relayed, self.ends = yr_g.at[k], yb_g.at[k]

        def ring(self):
            self.y.wait_recv()
            add_into(self.mine, self.got, 8)
            send(self.ap)
            send(self.am)

        def relay(self):
            self.ap.wait_recv()
            add_into(self.for_p, self.relayed.at[0], 1)
            send(self.bp)
            self.am.wait_recv()
            add_into(self.for_m, self.relayed.at[1], 1)
            send(self.bm)

        def total(self, i):
            v = self.last[i].astype(jnp.float32) + self.ends[0, i].astype(jnp.float32)
            return v + self.ends[1, i].astype(jnp.float32)

    def reduce_rows(buf, which, base):
        part = lambda j, r: buf.at[pl.ds((r * 2 + j) * 8, 8)]
        return Reduce(
            part, z, yl, dev_zp, dev_zm, dev_yl, ra_o.at[which], rb_o.at[which], rm_o.at[which], base
        )

    def build_lists():
        n, wide = CAP, 2 * B
        row_i = lax.broadcasted_iota(jnp.int32, (n, n), 0)
        lane_i = lax.broadcasted_iota(jnp.int32, (n, n), 1)
        eye = row_i == lane_i
        earlier = lane_i < row_i
        later = lane_i > row_i
        lane1 = lax.broadcasted_iota(jnp.int32, (1, n), 1)
        place = lax.broadcasted_iota(jnp.int32, (n, wide), 1)
        group = lax.broadcasted_iota(jnp.int32, (n, wide), 1)

        def flag(m):
            return jnp.where(m, 1, 0)

        def spread(row):
            return jnp.broadcast_to(row, (n, n))

        def column(row):
            return jnp.sum(jnp.where(eye, spread(row), 0), axis=1, keepdims=True)

        def items(k, target, source, source_base):
            alive = lane1 < counts[0, k]
            key = jnp.where(alive, index_v[k, target : target + 1, :], DB)
            src = index_v[k, source : source + 1, :] + source_base
            return key, lane1 + k * CAP + (src << 9)

        def one_list(which, sets):
            keys = [key for key, _ in sets]
            cols = [column(key) for key in keys]
            m = len(sets)
            odd_last = []
            for b in range(m):
                same = [flag(cols[a] == spread(keys[b])) for a in range(m)]
                count = sum(jnp.sum(s, axis=0, keepdims=True) for s in same)
                rank = jnp.sum(jnp.where(later, same[b], 0), axis=0, keepdims=True)
                for a in range(b):
                    rank = rank + jnp.sum(same[a], axis=0, keepdims=True)
                odd_last.append(jnp.where(rank + 1 == count, count & 1, 0))
            filled = jnp.zeros((1, wide), jnp.int32)
            taken = jnp.zeros((1, wide), jnp.int32)
            last = jnp.full((1, wide), -1, jnp.int32)
            for a in range(m):
                before = jnp.zeros((n, 1), jnp.int32)
                rank = jnp.zeros((n, 1), jnp.int32)
                for b in range(m):
                    less = spread(keys[b]) < cols[a]
                    weight = spread(1 + odd_last[b])
                    before = before + jnp.sum(jnp.where(less, weight, 0), axis=1, keepdims=True)
                    same = flag(spread(keys[b]) == cols[a])
                    if b == a:
                        same = jnp.where(earlier, same, 0)
                    if b <= a:
                        rank = rank + jnp.sum(same, axis=1, keepdims=True)
                at = before + rank
                packed = column(sets[a][1]) + jnp.where(rank >= 2, 65536, 0)
                hit = at == place
                filled = filled + jnp.sum(jnp.where(hit, packed, 0), axis=0, keepdims=True)
                taken = taken + jnp.sum(flag(hit), axis=0, keepdims=True)
                step = at >> 1
                mine = jnp.where(cols[a] == group, step, -1)
                last = jnp.maximum(last, jnp.max(mine, axis=0, keepdims=True))
            entry = jnp.where(taken > 0, filled, NO_SLOT)
            lists_v[which : which + 1, :] = entry
            last = jnp.where(last < 0, ZERO, last + BASE[which])
            lists_v[5 + which : 6 + which, :] = last

        local(index, index_v, L_IDX).wait()
        one_list(0, [items(0, 1, 0, 0)])
        one_list(1, [items(1, 1, 0, 0)])
        one_list(2, [items(2, 1, 0, 0)])
        one_list(3, [items(2, 0, 1, 0)])
        one_list(4, [items(0, 0, 1, 0), items(1, 0, 1, HB)])
        copy = local(lists_v, lists, L_LIST)
        copy.start()
        copy.wait()
        local(index, pairs, L_IDX + 1).wait()

    gx, gg = Gather(xb, R_X), Gather(gb, R_OG)
    for i in range(8):
        local(inputs.at[:, pl.ds(i * B, B)], xb.at[t * 8 + i], L_X + i).wait()
    send(gx.bp)
    send(gx.bm)
    send(gx.a)
    for i in range(8):
        local(out_grad.at[:, pl.ds(i * B, B)], gb.at[t * 8 + i], L_OG + i).wait()
    send(gg.bp)
    send(gg.bm)
    send(gg.a)
    build_lists()
    gx.bp.wait_recv()
    send(gx.dp)
    gx.bm.wait_recv()
    send(gx.dm)
    gx.a.wait_recv()
    send(gx.cp)
    send(gx.cm)
    gg.bp.wait_recv()
    send(gg.dp)
    gg.bm.wait_recv()
    send(gg.dm)
    gg.a.wait_recv()
    send(gg.cp)
    send(gg.cm)
    gx.dp.wait_recv()
    gx.dm.wait_recv()
    send(gx.e)
    for k in range(3):
        local(weights.at[k], wb.at[pl.ds(k * CAP, CAP)], L_W + k).wait()
    gx.cp.wait_recv()
    gx.cm.wait_recv()
    gx.e.wait_recv()

    acc = products(0, 0, 32, xb, False)(zero)
    gg.dp.wait_recv()
    gg.dm.wait_recv()
    send(gg.e)
    products(0, 32, PAIRS[0], xb, False)(acc)
    products(1, 0, PAIRS[1], xb, False)(zero)

    def forward(h, carry):
        g, u = sums[lists[5, h]], sums[lists[6, h]]
        gate[h], up[h] = g, u
        hidden[h] = (g * jax.nn.sigmoid(g) * u).astype(jnp.bfloat16)
        return carry

    lax.fori_loop(0, HB, forward, 0)

    products(3, 0, PAIRS[3], hidden, False)(zero)
    gather_blocks(3, ob)
    red_o = reduce_rows(ob, 0, R_O)
    red_o.start()
    red_o.more()
    gg.cp.wait_recv()
    gg.cm.wait_recv()
    gg.e.wait_recv()

    red_g = [reduce_grads(k) for k in range(3)]
    red_y = [PairFirst(k) for k in range(3)]

    def start_grads(k):
        core_add(k, 0)
        red_g[k].start()
        core_add(k, 1)
        send(red_y[k].y)
        core_add(k, 2)
        core_add(k, 3)
        red_g[k].more()
        core_add(k, 4)
        core_add(k, 5)

    slot_grads(2, 1 - core, hidden, gb, True, 0)
    core_send(2)
    slot_grads(2, core, hidden, gb, True, 0)
    start_grads(2)
    products(2, 0, PAIRS[2], gb, True)(zero)

    def backward(h, carry):
        g, u, hg = gate[h], up[h], sums[lists[7, h]]
        sig = jax.nn.sigmoid(g)
        rows[h] = (hg * u * sig * (1.0 + g * (1.0 - sig))).astype(jnp.bfloat16)
        rows[h + HB] = (hg * (g * sig)).astype(jnp.bfloat16)
        return carry

    lax.fori_loop(0, HB, backward, 0)
    red_o.relay()
    slot_grads(0, 1 - core, xb, rows, False, 0)
    core_send(0)
    red_g[2].relay()
    slot_grads(0, core, xb, rows, False, 0)
    red_y[2].ring()
    start_grads(0)
    acc = products(4, 0, 64, rows, True)(zero)
    red_y[2].relay()
    red_o.cross()
    products(4, 64, PAIRS[4], rows, True)(acc)
    gather_blocks(4, ib)
    red_i = reduce_rows(ib, 1, R_I)
    red_i.start()
    red_i.more()
    red_g[0].relay()
    red_g[2].cross()
    slot_grads(1, 1 - core, xb, rows, False, HB)
    core_send(1)
    red_y[0].ring()
    slot_grads(1, core, xb, rows, False, HB)
    start_grads(1)
    red_i.relay()
    red_o.m.wait_recv()

    def finish_rows(red, out):
        for i in range(8):
            out[:, i * B : (i + 1) * B] = red.total(i).astype(jnp.bfloat16)

    finish_rows(red_o, out_o)

    def finish_grads(k):
        red = red_g[k]
        count = counts[0, k]

        def update(source, shift, i, carry):
            g = source.total(i)
            i = i + shift
            alive = (d * 6 + i < count).astype(jnp.float32)
            m = 0.9 * mom[0, k, i] + 0.1 * g
            v = 0.95 * mom[1, k, i] + 0.05 * g * g
            out_u[k, i] = alive * m / (jnp.sqrt(v) + EPSILON)
            return carry

        lax.fori_loop(0, 2, functools.partial(update, red_y[k], 4), 0)
        red.m.wait_recv()
        lax.fori_loop(0, 4, functools.partial(update, red, 0), 0)

    def end_pair_first(k):
        red_y[k].bp.wait_recv()
        red_y[k].bm.wait_recv()

    local(first, mom.at[0], L_M).wait()
    local(second, mom.at[1], L_M + 1).wait()
    red_y[0].relay()
    end_pair_first(2)
    finish_grads(2)
    red_g[0].cross()
    red_g[1].relay()
    red_y[1].ring()
    red_i.cross()
    end_pair_first(0)
    finish_grads(0)
    red_y[1].relay()
    red_i.m.wait_recv()
    finish_rows(red_i, out_i)
    red_g[1].cross()
    end_pair_first(1)
    finish_grads(1)
    for copy in sent:
        copy.wait_send()


def store(*refs):
    src, dst, sem = refs[:3], refs[3:6], refs[6]
    copies = [pltpu.make_async_copy(s, o, sem.at[i]) for i, (s, o) in enumerate(zip(src, dst))]
    for copy in copies:
        copy.start()
    for copy in copies:
        copy.wait()


def local_step(inputs, out_grad, weights, block_index, block_counts, first_moment, second_moment):
    index = jnp.transpose(block_index, (0, 2, 1))
    any_, smem, vmem = (
        pl.BlockSpec(memory_space=s) for s in (pl.ANY, pltpu.SMEM, pltpu.VMEM)
    )
    f32, bf16, i32 = jnp.float32, jnp.bfloat16, jnp.int32
    blocks = lambda *n, dtype=bf16: pltpu.VMEM((*n, B, B), dtype)
    dma = pltpu.SemaphoreType.DMA
    shapes = (
        jax.ShapeDtypeStruct(inputs.shape, bf16),
        jax.ShapeDtypeStruct(inputs.shape, bf16),
        jax.ShapeDtypeStruct(first_moment.shape, f32),
    )
    results = pl.pallas_call(
        kernel,
        out_shape=shapes,
        in_specs=[any_, any_, any_, any_, smem, any_, any_],
        out_specs=[vmem, vmem, vmem],
        scratch_shapes=[
            blocks(DB),
            blocks(DB),
            blocks(3 * CAP + 1),
            blocks(ZERO + 1, dtype=f32),
            blocks(HB, dtype=f32),
            blocks(HB, dtype=f32),
            blocks(HB),
            blocks(2 * HB),
            blocks(DB),
            blocks(DB),
            blocks(2, 3 * 48),
            blocks(3 * 48),
            blocks(2, 2, 8),
            blocks(2, 2, 2, 8),
            blocks(2, 8),
            blocks(3, 2, 4),
            blocks(3, 2, 2, 4),
            blocks(3, 4),
            blocks(3, 8),
            blocks(3, 2, 1),
            blocks(3, 2, 2),
            blocks(2, 3, 6, dtype=f32),
            pltpu.VMEM((3, 2, CAP), i32),
            pltpu.SMEM((3, 2, CAP), i32),
            pltpu.VMEM((16, 2 * B), i32),
            pltpu.SMEM((16, 2 * B), i32),
            dma((N_LOCAL,)),
            dma((N_REMOTE,)),
            dma((N_REMOTE,)),
        ],
        compiler_params=pltpu.CompilerParams(
            collective_id=0, has_side_effects=True, vmem_limit_bytes=63_000_000
        ),
    )(inputs, out_grad, weights, index, block_counts, first_moment, second_moment)
    return pl.pallas_call(
        store,
        out_shape=shapes,
        in_specs=[vmem, vmem, vmem],
        out_specs=[any_, any_, any_],
        scratch_shapes=[dma((3,))],
    )(*results)


def solution(mesh):
    in_specs = (
        P("dp", "tensor"),
        P("dp", "tensor"),
        P(None, "tensor", None, None),
        P(None, "tensor", None),
        P("tensor", None),
        P(None, ("tensor", "dp"), None, None),
        P(None, ("tensor", "dp"), None, None),
    )
    out_specs = (P("dp", "tensor"), P("dp", "tensor"), P(None, ("tensor", "dp"), None, None))
    return jax.shard_map(local_step, mesh=mesh, in_specs=in_specs, out_specs=out_specs, check_vma=False)
```

time: 126 us -> 97.6 us (0.77)
  Pallas kernels: 113 us -> 96.8 us
  local copies, waits for them, and re-layouts: 7.3 us -> 0 us
  other arithmetic: 5.25 us -> 0 us
    pallas_call x1 -> x2, Pallas kernels: 113 us -> 96.8 us  [the longest x1 94.1 us: local_step(): pl.pallas_call(kernel, out_shape=shapes, in_specs=[any_, any_, any_, any_...]
    unnamed x3 -> x0, local copies, waits for them, and re-layouts: 5.72 us -> none
    or x4 -> x0, other arithmetic: 2.11 us -> none  [the longest x2 0.85 us: padded(): packed = weight | source << 9 | jnp.where(alive, target, DB) << 16]
    select_n x1 -> x0, other arithmetic: 1.32 us -> none  [slot_lists(): lasts = jnp.where(upto > before, upto - 1 + base[:, None], ZERO)]
where the time goes in v1:
time: 97.6 us; the launch traced here: 97.4 us
  Pallas kernels  96.8 us (99%)
    pallas_call x1, Pallas kernels, local_step(): pl.pallas_call(kernel, out_shape=shapes, in_specs=[any_, any_, any_, any_...  94.1 us
    pallas_call x1, Pallas kernels, local_step(): pl.pallas_call(store, out_shape=shapes, in_specs=[vmem, vmem, vmem], out_...  2.65 us

profile of v1, /device:TPU:0, one launch (start us, length us, event | category | flops | bytes accessed | tf_op | source)
XLA Modules:
  0.0 97.4 jit_solution(14625832088943364925)
XLA Ops:
  0.6 94.1 %shard_map.94 = (bf16[128,1024]{1,0:T(8,128)(2,1)}, bf16[128,1024]{1,0:T(8,128)(2,1)}, f32[3,6,128,128]{3,2,1,0:T(8,128)}) custom-call(bf16[128,1024]{1,0:T(8,128)(2,1)} %inputs.1, bf16[128,1024]{1,0:T(8,128)(2,1)} %out_grad.1, bf16[3,96,128,128]{3,2,1,0:T(8,128)(2,1)} %weights.1, s32[3,2,96]{2,1,0:T(2,128)} %bitcast.1, s32[1,3]{1,0:T(1,128)} %counts.1, ...), custom_call_target="tpu_custom_call" | custom-call | tf_op jit(solution)/shard_map/pallas_call | solution.py:513
  94.8 2.7 %shard_map.95 = (bf16[128,1024]{1,0:T(8,128)(2,1)}, bf16[128,1024]{1,0:T(8,128)(2,1)}, f32[3,6,128,128]{3,2,1,0:T(8,128)}) custom-call(bf16[128,1024]{1,0:T(8,128)(2,1)} %get-tuple-element.6.refs_0_, bf16[128,1024]{1,0:T(8,128)(2,1)} %get-tuple-element.7.refs_1_, f32[3,6,128,128]{3,2,1,0:T(8,128)} %get-tuple-element.8.refs_2_), custom_call_target="tpu_custom_call" | custom-call | tf_op jit(solution)/shard_map/pallas_call | solution.py:553

commit v2 on v1

--- a/solution.py
+++ b/solution.py
@@ -14,6 +14,7 @@
 DB = 64
 B = 128
 PAIRS = (56, 56, 56, 80, 128)
+UNROLL = (28, 28, 28, 20, 32)
 BASE = (0, 64, 64, 0, 0)
 ZERO = 128
 NO_SLOT = 3 * CAP
@@ -65,10 +66,6 @@
     barrier = pltpu.get_barrier_semaphore()
     for dev in (dev_core, dev_xp, dev_xm, dev_yh, dev_zp, dev_zm, dev_yl):
         pl.semaphore_signal(barrier, inc=1, device_id=dev, device_id_type=MESH)
-    for k in range(3):
-        local(weights.at[k], wb.at[pl.ds(k * CAP, CAP)], L_W + k).start()
-    local(first, mom.at[0], L_M).start()
-    local(second, mom.at[1], L_M + 1).start()
     local(index, index_v, L_IDX).start()
     local(index, pairs, L_IDX + 1).start()
     wb[NO_SLOT] = jnp.zeros((B, B), jnp.bfloat16)
@@ -126,12 +123,9 @@
             far = 1 - self.pair
             mine = self.part(far, self.pos)
 
-            def body(i, carry):
+            for i in range(self.n):
                 v = mine[i].astype(jnp.float32) + self.rb[0, far, i].astype(jnp.float32)
                 mine[i] = (v + self.rb[1, far, i].astype(jnp.float32)).astype(jnp.bfloat16)
-                return carry
-
-            lax.fori_loop(0, self.n, body, 0)
             send(self.m)
 
         def total(self, i):
@@ -141,15 +135,12 @@
             return v + self.rm[i].astype(jnp.float32)
 
     def add_into(dst, src, n):
-        def body(i, carry):
+        for i in range(n):
             dst[i] = (dst[i].astype(jnp.float32) + src[i].astype(jnp.float32)).astype(jnp.bfloat16)
-            return carry
-
-        lax.fori_loop(0, n, body, 0)
 
     def products(which, lo, hi, left, back):
         dims = (((1,), (1,)), ((), ())) if back else (((1,), (0,)), ((), ()))
-        unroll, base = 8, BASE[which]
+        unroll, base = UNROLL[which], BASE[which]
 
         def body(i, acc):
             for u in range(unroll):
@@ -174,32 +165,38 @@
             dst[i] = sums[lists[5 + which, i]].astype(jnp.bfloat16)
             return carry
 
-        lax.fori_loop(0, DB, body, 0, unroll=4)
-
-    def slot_grads(k, parity, left, right, left_hidden, row_base):
-        def body(b, carry):
-            x, y = b // 2, b % 2
-            s0 = (y * 8 + x * 2 + parity) * 6
-            for u in range(6):
-                f, h = pairs[k, 0, s0 + u], pairs[k, 1, s0 + u]
-                i, j = (h, f) if left_hidden else (f, h + row_base)
+        lax.fori_loop(0, DB, body, 0, unroll=16)
+
+    def piece_of(n):
+        nxt, opp, prv = (px + 1) % 4, (px + 2) % 4, (px + 3) % 4
+        ring = (opp, None, nxt, prv, None, px)[n]
+        pair = (None, 1 - yh, None, None, yh, None)[n]
+        return ring, pair, ring * 8 if pair is None else 32 + pair * 8
+
+    def slot_grads(k, parity, pieces):
+        left, right, left_hidden, row_base = (
+            (xb, rows, False, 0), (xb, rows, False, HB), (hidden, gb, True, 0)
+        )[k]
+        for n in pieces:
+            ring, pair, block = piece_of(n)
+            for i in range(8):
+                if pair is None:
+                    slot = ((i // 4) * 8 + ring * 2 + parity) * 6 + i % 4
+                else:
+                    slot = (pair * 8 + (i // 2) * 2 + parity) * 6 + 4 + i % 2
+                f, h = pairs[k, 0, slot], pairs[k, 1, slot]
+                li, ri = (h, f) if left_hidden else (f, h + row_base)
                 g = lax.dot_general(
-                    left[i], right[j], (((0,), (0,)), ((), ())), preferred_element_type=jnp.float32
+                    left[li], right[ri], (((0,), (0,)), ((), ())), preferred_element_type=jnp.float32
                 )
-                at = b * 4 + u if u < 4 else 28 + (y * 4 + x) * 2 + u
-                grads[parity, k * 48 + at] = g.astype(jnp.bfloat16)
-            return carry
-
-        lax.fori_loop(0, 8, body, 0)
+                grads[parity, k * 48 + block + i] = g.astype(jnp.bfloat16)
 
     def core_piece(k, n):
-        nxt, opp, prv = (px + 1) % 4, (px + 2) % 4, (px + 3) % 4
-        first_block = (opp * 8, 32 + (1 - yh) * 8, nxt * 8, prv * 8, 32 + yh * 8, px * 8)[n]
-        at = pl.ds(k * 48 + first_block, 8)
+        at = pl.ds(k * 48 + piece_of(n)[2], 8)
         return remote(grads.at[1 - core, at], core_in.at[at], R_CORE + k * 6 + n, dev_core), at
 
-    def core_send(k):
-        for n in range(6):
+    def core_send(k, pieces):
+        for n in pieces:
             send(core_piece(k, n)[0])
 
     def core_add(k, n):
@@ -339,35 +336,38 @@
     send(gg.bp)
     send(gg.bm)
     send(gg.a)
+    for k in range(3):
+        local(weights.at[k], wb.at[pl.ds(k * CAP, CAP)], L_W + k).start()
+    local(first, mom.at[0], L_M).start()
+    local(second, mom.at[1], L_M + 1).start()
     build_lists()
     gx.bp.wait_recv()
     send(gx.dp)
     gx.bm.wait_recv()
     send(gx.dm)
-    gx.a.wait_recv()
-    send(gx.cp)
-    send(gx.cm)
     gg.bp.wait_recv()
     send(gg.dp)
     gg.bm.wait_recv()
     send(gg.dm)
+    gx.a.wait_recv()
+    send(gx.cp)
+    send(gx.cm)
     gg.a.wait_recv()
     send(gg.cp)
     send(gg.cm)
     gx.dp.wait_recv()
     gx.dm.wait_recv()
     send(gx.e)
+    gg.dp.wait_recv()
+    gg.dm.wait_recv()
+    send(gg.e)
     for k in range(3):
         local(weights.at[k], wb.at[pl.ds(k * CAP, CAP)], L_W + k).wait()
     gx.cp.wait_recv()
     gx.cm.wait_recv()
     gx.e.wait_recv()
 
-    acc = products(0, 0, 32, xb, False)(zero)
-    gg.dp.wait_recv()
-    gg.dm.wait_recv()
-    send(gg.e)
-    products(0, 32, PAIRS[0], xb, False)(acc)
+    products(0, 0, PAIRS[0], xb, False)(zero)
     products(1, 0, PAIRS[1], xb, False)(zero)
 
     def forward(h, carry):
@@ -390,21 +390,30 @@
     red_g = [reduce_grads(k) for k in range(3)]
     red_y = [PairFirst(k) for k in range(3)]
 
-    def start_grads(k):
+    def head(k):
+        slot_grads(k, 1 - core, (0, 1))
+        core_send(k, (0, 1))
+        slot_grads(k, core, (0, 1))
+        slot_grads(k, 1 - core, (2, 3))
+        core_send(k, (2, 3))
         core_add(k, 0)
         red_g[k].start()
         core_add(k, 1)
         send(red_y[k].y)
+
+    def tail(k):
+        slot_grads(k, core, (2, 3))
+        slot_grads(k, 1 - core, (4, 5))
+        core_send(k, (4, 5))
         core_add(k, 2)
         core_add(k, 3)
         red_g[k].more()
+        slot_grads(k, core, (4, 5))
         core_add(k, 4)
         core_add(k, 5)
 
-    slot_grads(2, 1 - core, hidden, gb, True, 0)
-    core_send(2)
-    slot_grads(2, core, hidden, gb, True, 0)
-    start_grads(2)
+    head(2)
+    tail(2)
     products(2, 0, PAIRS[2], gb, True)(zero)
 
     def backward(h, carry):
@@ -415,36 +424,28 @@
         return carry
 
     lax.fori_loop(0, HB, backward, 0)
+    head(0)
+    red_g[2].relay()
+    tail(0)
+    red_y[2].ring()
     red_o.relay()
-    slot_grads(0, 1 - core, xb, rows, False, 0)
-    core_send(0)
-    red_g[2].relay()
-    slot_grads(0, core, xb, rows, False, 0)
-    red_y[2].ring()
-    start_grads(0)
-    acc = products(4, 0, 64, rows, True)(zero)
-    red_y[2].relay()
-    red_o.cross()
-    products(4, 64, PAIRS[4], rows, True)(acc)
+    products(4, 0, PAIRS[4], rows, True)(zero)
     gather_blocks(4, ib)
     red_i = reduce_rows(ib, 1, R_I)
     red_i.start()
     red_i.more()
+    red_g[2].cross()
+    head(1)
     red_g[0].relay()
-    red_g[2].cross()
-    slot_grads(1, 1 - core, xb, rows, False, HB)
-    core_send(1)
+    red_y[2].relay()
+    tail(1)
     red_y[0].ring()
-    slot_grads(1, core, xb, rows, False, HB)
-    start_grads(1)
-    red_i.relay()
-    red_o.m.wait_recv()
+    red_o.cross()
 
     def finish_rows(red, out):
         for i in range(8):
             out[:, i * B : (i + 1) * B] = red.total(i).astype(jnp.bfloat16)
 
-    finish_rows(red_o, out_o)
 
     def finish_grads(k):
         red = red_g[k]
@@ -469,21 +470,24 @@
 
     local(first, mom.at[0], L_M).wait()
     local(second, mom.at[1], L_M + 1).wait()
-    red_y[0].relay()
     end_pair_first(2)
     finish_grads(2)
+    red_y[0].relay()
+    red_y[1].ring()
+    red_i.relay()
+    red_g[1].relay()
     red_g[0].cross()
-    red_g[1].relay()
-    red_y[1].ring()
-    red_i.cross()
+    red_o.m.wait_recv()
+    finish_rows(red_o, out_o)
+    red_y[1].relay()
     end_pair_first(0)
     finish_grads(0)
-    red_y[1].relay()
+    red_g[1].cross()
+    red_i.cross()
+    end_pair_first(1)
+    finish_grads(1)
     red_i.m.wait_recv()
     finish_rows(red_i, out_i)
-    red_g[1].cross()
-    end_pair_first(1)
-    finish_grads(1)
     for copy in sent:
         copy.wait_send()
 

time: 97.6 us -> 91.2 us (0.934)
  Pallas kernels: 96.8 us -> 90.4 us
    pallas_call x1, Pallas kernels: 94.1 us -> 87.7 us  [local_step(): pl.pallas_call(kernel, out_shape=shapes, in_specs=[any_, any_, any_, any_...]
where the time goes in v2:
time: 91.2 us; the launch traced here: 91 us
  Pallas kernels  90.4 us (99%)
    pallas_call x1, Pallas kernels, local_step(): pl.pallas_call(kernel, out_shape=shapes, in_specs=[any_, any_, any_, any_...  87.7 us
    pallas_call x1, Pallas kernels, local_step(): pl.pallas_call(store, out_shape=shapes, in_specs=[vmem, vmem, vmem], out_...  2.65 us

profile of v2, /device:TPU:0, one launch (start us, length us, event | category | flops | bytes accessed | tf_op | source)
XLA Modules:
  0.0 91.0 jit_solution(8509483892172337127)
XLA Ops:
  0.6 87.7 %shard_map.94 = (bf16[128,1024]{1,0:T(8,128)(2,1)}, bf16[128,1024]{1,0:T(8,128)(2,1)}, f32[3,6,128,128]{3,2,1,0:T(8,128)}) custom-call(bf16[128,1024]{1,0:T(8,128)(2,1)} %inputs.1, bf16[128,1024]{1,0:T(8,128)(2,1)} %out_grad.1, bf16[3,96,128,128]{3,2,1,0:T(8,128)(2,1)} %weights.1, s32[3,2,96]{2,1,0:T(2,128)} %bitcast.1, s32[1,3]{1,0:T(1,128)} %counts.1, ...), custom_call_target="tpu_custom_call" | custom-call | tf_op jit(solution)/shard_map/pallas_call | solution.py:517
  88.4 2.7 %shard_map.95 = (bf16[128,1024]{1,0:T(8,128)(2,1)}, bf16[128,1024]{1,0:T(8,128)(2,1)}, f32[3,6,128,128]{3,2,1,0:T(8,128)}) custom-call(bf16[128,1024]{1,0:T(8,128)(2,1)} %get-tuple-element.6.refs_0_, bf16[128,1024]{1,0:T(8,128)(2,1)} %get-tuple-element.7.refs_1_, f32[3,6,128,128]{3,2,1,0:T(8,128)} %get-tuple-element.8.refs_2_), custom_call_target="tpu_custom_call" | custom-call | tf_op jit(solution)/shard_map/pallas_call | solution.py:557

commit v3 on v2

--- a/solution.py
+++ b/solution.py
@@ -441,6 +441,10 @@
     tail(1)
     red_y[0].ring()
     red_o.cross()
+    red_g[1].relay()
+    red_y[1].ring()
+    red_i.relay()
+    red_g[0].cross()
 
     def finish_rows(red, out):
         for i in range(8):
@@ -470,20 +474,16 @@
 
     local(first, mom.at[0], L_M).wait()
     local(second, mom.at[1], L_M + 1).wait()
+    red_y[0].relay()
+    red_o.m.wait_recv()
+    finish_rows(red_o, out_o)
     end_pair_first(2)
     finish_grads(2)
-    red_y[0].relay()
-    red_y[1].ring()
-    red_i.relay()
-    red_g[1].relay()
-    red_g[0].cross()
-    red_o.m.wait_recv()
-    finish_rows(red_o, out_o)
     red_y[1].relay()
+    red_g[1].cross()
+    red_i.cross()
     end_pair_first(0)
     finish_grads(0)
-    red_g[1].cross()
-    red_i.cross()
     end_pair_first(1)
     finish_grads(1)
     red_i.m.wait_recv()

time: 91.2 us -> 88.7 us (0.973)
  Pallas kernels: 90.4 us -> 87.9 us
    pallas_call x1, Pallas kernels: 87.7 us -> 85.2 us  [local_step(): pl.pallas_call(kernel, out_shape=shapes, in_specs=[any_, any_, any_, any_...]
where the time goes in v3:
time: 88.7 us; the launch traced here: 88.5 us
  Pallas kernels  87.9 us (99%)
    pallas_call x1, Pallas kernels, local_step(): pl.pallas_call(kernel, out_shape=shapes, in_specs=[any_, any_, any_, any_...  85.2 us
    pallas_call x1, Pallas kernels, local_step(): pl.pallas_call(store, out_shape=shapes, in_specs=[vmem, vmem, vmem], out_...  2.65 us

profile of v3, /device:TPU:0, one launch (start us, length us, event | category | flops | bytes accessed | tf_op | source)
XLA Modules:
  0.0 88.5 jit_solution(7235726714802368790)
XLA Ops:
  0.6 85.2 %shard_map.94 = (bf16[128,1024]{1,0:T(8,128)(2,1)}, bf16[128,1024]{1,0:T(8,128)(2,1)}, f32[3,6,128,128]{3,2,1,0:T(8,128)}) custom-call(bf16[128,1024]{1,0:T(8,128)(2,1)} %inputs.1, bf16[128,1024]{1,0:T(8,128)(2,1)} %out_grad.1, bf16[3,96,128,128]{3,2,1,0:T(8,128)(2,1)} %weights.1, s32[3,2,96]{2,1,0:T(2,128)} %bitcast.1, s32[1,3]{1,0:T(1,128)} %counts.1, ...), custom_call_target="tpu_custom_call" | custom-call | tf_op jit(solution)/shard_map/pallas_call | solution.py:517
  85.9 2.7 %shard_map.95 = (bf16[128,1024]{1,0:T(8,128)(2,1)}, bf16[128,1024]{1,0:T(8,128)(2,1)}, f32[3,6,128,128]{3,2,1,0:T(8,128)}) custom-call(bf16[128,1024]{1,0:T(8,128)(2,1)} %get-tuple-element.6.refs_0_, bf16[128,1024]{1,0:T(8,128)(2,1)} %get-tuple-element.7.refs_1_, f32[3,6,128,128]{3,2,1,0:T(8,128)} %get-tuple-element.8.refs_2_), custom_call_target="tpu_custom_call" | custom-call | tf_op jit(solution)/shard_map/pallas_call | solution.py:557
